TPU v7x, 32 devices: a whole 2x2x4 slice. The times are simulated.
32 devices in a mesh: dp: 8 (over z, y), tensor: 4 (over x, core).
Axes of the slice: x: 2, y: 2, z: 4, core: 2. Of those that a mesh axis runs over, the one named last changes fastest.
Arguments:
- tokens: bfloat16 [8, 1536, 768], P('dp'), may hold values from -6 to 6
- timesteps: int32 [8], P('dp'), may hold values from 0 to 999
- piece_starts: int32 [8, 3], P('dp'), may hold values from 0 to 1280, as said below
- step_table: bfloat16 [1000, 768], replicated, may hold values from -4 to 4
- first_gain: float32 [768], replicated, may hold values from 0.5 to 1.5
- first_shift: float32 [768], replicated, may hold values from -2 to 2
- w_query: bfloat16 [768, 768], P(None, 'tensor'), may hold values from -0.3125 to 0.3125
- b_query: float32 [768], P('tensor'), may hold values from -2 to 2
- w_key: bfloat16 [768, 768], P(None, 'tensor'), may hold values from -0.3125 to 0.3125
- w_value: bfloat16 [768, 768], P(None, 'tensor'), may hold values from -0.21875 to 0.21875
- b_value: float32 [768], P('tensor'), may hold values from -2 to 2
- w_out: bfloat16 [768, 768], P('tensor'), may hold values from -0.875 to 0.875
- b_out: float32 [768], replicated, may hold values from -2 to 2
- second_gain: float32 [768], replicated, may hold values from 0.5 to 1.5
- second_shift: float32 [768], replicated, may hold values from -2 to 2
- w_in: bfloat16 [768, 3072], P(None, 'tensor'), may hold values from -0.21875 to 0.21875
- b_in: float32 [3072], P('tensor'), may hold values from -2 to 2
- w_down: bfloat16 [3072, 768], P('tensor'), may hold values from -0.109375 to 0.109375
- b_down: float32 [768], replicated, may hold values from -2 to 2
- cotangent: bfloat16 [8, 1536, 768], P('dp'), may hold values from -6 to 6
Outputs:
- output: bfloat16 [8, 1536, 768], P('dp')
- grad_tokens: bfloat16 [8, 1536, 768], P('dp')
- grad_step_table: float32 [1000, 768], replicated
- grad_first_gain: float32 [768], replicated
- grad_first_shift: float32 [768], replicated
- grad_w_query: float32 [768, 768], P(None, 'tensor')
- grad_b_query: float32 [768], P('tensor')
- grad_w_key: float32 [768, 768], P(None, 'tensor')
- grad_w_value: float32 [768, 768], P(None, 'tensor')
- grad_b_value: float32 [768], P('tensor')
- grad_w_out: float32 [768, 768], P('tensor')
- grad_b_out: float32 [768], replicated
- grad_second_gain: float32 [768], replicated
- grad_second_shift: float32 [768], replicated
- grad_w_in: float32 [768, 3072], P(None, 'tensor')
- grad_b_in: float32 [3072], P('tensor')
- grad_w_down: float32 [3072, 768], P('tensor')
- grad_b_down: float32 [768], replicated
Inputs may be any that keep to these rules, and one draw needn't show every extreme that they name: `piece_starts`: piece k of a sequence starts between 2 * k * 256 and 2 * k * 256 + 256, so pieces of 256 tokens lie inside their sequence, in order, without intersection.
All inputs are finite; a program needn't handle non-finite values.
Results may differ from a plain program's by a relative error of at most 0.02.
Values may be sent and summed in bfloat16 or wider, within the bound.
No kernel may reach another device: no remote copies, remote signals or barrier semaphores. Data moves between devices by JAX's collectives and lax.ppermute only.
A program may use at most 128 MiB of HBM per device.

v0:
```python
import jax
import jax.numpy as jnp
from jax import lax
from jax.sharding import PartitionSpec as P

HD = 64
PIECE = 256
QB = 512
EPS = 1e-05


def inner_rows(left, right):
    return lax.dot_general(
        left, right, (((0,), (0,)), ((), ())), preferred_element_type=jnp.float32
    )


def times_trans(left, right):
    return lax.dot_general(
        left, right, (((1,), (1,)), ((), ())), preferred_element_type=jnp.float32
    )


def normalize(values, gain, shift):
    center = values - jnp.mean(values, axis=-1, keepdims=True)
    root = lax.rsqrt(jnp.mean(center * center, axis=-1, keepdims=True) + EPS)
    hat = center * root
    return (hat * gain + shift, hat, root)


def norm_back(grad_in, hat, root, gain):
    scaled = grad_in * gain
    return root * (
        scaled
        - jnp.mean(scaled, axis=-1, keepdims=True)
        - hat * jnp.mean(scaled * hat, axis=-1, keepdims=True)
    )


def piece_labels(starts, length):
    positions = jnp.arange(length, dtype=jnp.int32)
    inside = (positions[None, :] >= starts[:, None]) & (
        positions[None, :] < starts[:, None] + PIECE
    )
    numbers = jnp.arange(1, starts.shape[0] + 1, dtype=jnp.int32)
    return jnp.sum(jnp.where(inside, numbers[:, None], 0), axis=0)


def block_scores(query_block, keys3, labels_q, place_q, labels, positions):
    scores = jnp.einsum("qhd,khd->hqk", query_block, keys3, preferred_element_type=jnp.float32)
    allowed = (positions[None, :] <= place_q[:, None]) | (labels_q[:, None] == labels[None, :]) & (
        labels_q[:, None] > 0
    )
    return jnp.where(allowed[None], scores, -1e30)


def per_device(
    tokens,
    timesteps,
    piece_starts,
    step_table,
    first_gain,
    first_shift,
    w_query,
    b_query,
    w_key,
    w_value,
    b_value,
    w_out,
    b_out,
    second_gain,
    second_shift,
    w_in,
    b_in,
    w_down,
    b_down,
    cotangent,
):
    length = tokens.shape[1]
    heads_here = w_query.shape[1] // HD
    scale = HD ** (-0.5)
    nblocks = length // QB
    table_rows = step_table.shape[0]
    onehot = (jnp.arange(table_rows, dtype=jnp.int32) == timesteps[0]).astype(jnp.bfloat16)
    step_row = jnp.dot(onehot[None, :], step_table, preferred_element_type=jnp.float32)[0]
    stream = tokens[0].astype(jnp.float32) + step_row[None, :]
    first_out, hat_one, root_one = normalize(stream, first_gain, first_shift)
    normed_one = first_out.astype(jnp.bfloat16)
    queries = (
        (jnp.dot(normed_one, w_query, preferred_element_type=jnp.float32) + b_query) * scale
    ).astype(jnp.bfloat16)
    keys_b = jnp.dot(normed_one, w_key, preferred_element_type=jnp.float32).astype(jnp.bfloat16)
    values_b = (jnp.dot(normed_one, w_value, preferred_element_type=jnp.float32) + b_value).astype(
        jnp.bfloat16
    )
    positions = jnp.arange(length, dtype=jnp.int32)
    labels = piece_labels(piece_starts[0], length)
    query_blocks = queries.reshape(nblocks, QB, heads_here, HD)
    keys3 = keys_b.reshape(length, heads_here, HD)
    values3 = values_b.reshape(length, heads_here, HD)
    label_blocks = labels.reshape(nblocks, QB)
    place_blocks = positions.reshape(nblocks, QB)

    def forward_block(pieces):
        query_block, labels_q, place_q = pieces
        scores = block_scores(query_block, keys3, labels_q, place_q, labels, positions)
        top = jnp.max(scores, axis=-1, keepdims=True)
        weights = jnp.exp(scores - top)
        total = jnp.sum(weights, axis=-1, keepdims=True)
        probs_b = (weights / total).astype(jnp.bfloat16)
        mixed = jnp.einsum("hqk,khd->qhd", probs_b, values3, preferred_element_type=jnp.float32)
        return (mixed.astype(jnp.bfloat16), (top + jnp.log(total))[:, :, 0])

    mixed_blocks, log_totals = lax.map(forward_block, (query_blocks, label_blocks, place_blocks))
    mixed_flat = mixed_blocks.reshape(length, heads_here * HD)
    attn_part = jnp.dot(mixed_flat, w_out, preferred_element_type=jnp.float32)
    attn = lax.psum(attn_part.astype(jnp.bfloat16), "tensor").astype(jnp.float32) + b_out
    hidden_one = stream + attn
    second_out, hat_two, root_two = normalize(hidden_one, second_gain, second_shift)
    normed_two = second_out.astype(jnp.bfloat16)
    pre_act = jnp.dot(normed_two, w_in, preferred_element_type=jnp.float32) + b_in
    active = jax.nn.gelu(pre_act, approximate=True).astype(jnp.bfloat16)
    mlp_part = jnp.dot(active, w_down, preferred_element_type=jnp.float32)
    mlp = lax.psum(mlp_part.astype(jnp.bfloat16), "tensor").astype(jnp.float32) + b_down
    output = (hidden_one + mlp).astype(jnp.bfloat16)[None]
    grad_top = cotangent[0]
    grad_top_f = grad_top.astype(jnp.float32)
    g_b_down = jnp.sum(grad_top_f, axis=0)
    g_w_down = inner_rows(active, grad_top)
    grad_active = times_trans(grad_top, w_down)
    _, gelu_pull = jax.vjp(lambda value: jax.nn.gelu(value, approximate=True), pre_act)
    grad_pre = gelu_pull(grad_active)[0].astype(jnp.bfloat16)
    g_b_in = jnp.sum(grad_pre.astype(jnp.float32), axis=0)
    g_w_in = inner_rows(normed_two, grad_pre)
    grad_two = lax.psum(times_trans(grad_pre, w_in).astype(jnp.bfloat16), "tensor").astype(
        jnp.float32
    )
    g_second_gain = jnp.sum(grad_two * hat_two, axis=0)
    g_second_shift = jnp.sum(grad_two, axis=0)
    g_w_in, g_b_in, g_w_down, g_b_down, g_second_gain, g_second_shift = lax.psum(
        (g_w_in, g_b_in, g_w_down, g_b_down, g_second_gain, g_second_shift), "dp"
    )
    grad_hidden = grad_top_f + norm_back(grad_two, hat_two, root_two, second_gain)
    grad_hidden_b = grad_hidden.astype(jnp.bfloat16)
    g_b_out = jnp.sum(grad_hidden, axis=0)
    g_w_out = inner_rows(mixed_flat, grad_hidden_b)
    grad_mixed = times_trans(grad_hidden_b, w_out).astype(jnp.bfloat16)
    grad_mixed_blocks = grad_mixed.reshape(nblocks, QB, heads_here, HD)

    def backward_block(carry, pieces):
        acc_keys, acc_values = carry
        query_block, labels_q, place_q, log_total, grad_block = pieces
        scores = block_scores(query_block, keys3, labels_q, place_q, labels, positions)
        probs = jnp.exp(scores - log_total[:, :, None])
        probs_b = probs.astype(jnp.bfloat16)
        grad_probs = jnp.einsum(
            "qhd,khd->hqk", grad_block, values3, preferred_element_type=jnp.float32
        )
        centre = jnp.sum(probs * grad_probs, axis=-1, keepdims=True)
        grad_scores = (probs * (grad_probs - centre)).astype(jnp.bfloat16)
        grad_query = jnp.einsum(
            "hqk,khd->qhd", grad_scores, keys3, preferred_element_type=jnp.float32
        )
        acc_keys = acc_keys + jnp.einsum(
            "hqk,qhd->khd", grad_scores, query_block, preferred_element_type=jnp.float32
        )
        acc_values = acc_values + jnp.einsum(
            "hqk,qhd->khd", probs_b, grad_block, preferred_element_type=jnp.float32
        )
        return ((acc_keys, acc_values), grad_query.astype(jnp.bfloat16))

    zero_acc = jnp.zeros((length, heads_here, HD), jnp.float32)
    (acc_keys, acc_values), grad_query_blocks = lax.scan(
        backward_block,
        (zero_acc, zero_acc),
        (query_blocks, label_blocks, place_blocks, log_totals, grad_mixed_blocks),
    )
    grad_queries = grad_query_blocks.reshape(length, heads_here * HD) * scale
    grad_keys = acc_keys.reshape(length, heads_here * HD).astype(jnp.bfloat16)
    grad_values = acc_values.reshape(length, heads_here * HD).astype(jnp.bfloat16)
    g_b_query = jnp.sum(grad_queries.astype(jnp.float32), axis=0)
    g_b_value = jnp.sum(grad_values.astype(jnp.float32), axis=0)
    g_w_query = inner_rows(normed_one, grad_queries)
    g_w_key = inner_rows(normed_one, grad_keys)
    g_w_value = inner_rows(normed_one, grad_values)
    grad_one_part = (
        times_trans(grad_queries, w_query)
        + times_trans(grad_keys, w_key)
        + times_trans(grad_values, w_value)
    )
    grad_one = lax.psum(grad_one_part.astype(jnp.bfloat16), "tensor").astype(jnp.float32)
    g_first_gain = jnp.sum(grad_one * hat_one, axis=0)
    g_first_shift = jnp.sum(grad_one, axis=0)
    grad_stream = grad_hidden + norm_back(grad_one, hat_one, root_one, first_gain)
    grad_tokens = grad_stream.astype(jnp.bfloat16)[None]
    row_total = jnp.sum(grad_stream, axis=0)
    table_local = onehot.astype(jnp.float32)[:, None] * row_total[None, :]
    (
        g_w_query,
        g_b_query,
        g_w_key,
        g_w_value,
        g_b_value,
        g_w_out,
        g_b_out,
        g_first_gain,
        g_first_shift,
        g_table,
    ) = lax.psum(
        (
            g_w_query,
            g_b_query,
            g_w_key,
            g_w_value,
            g_b_value,
            g_w_out,
            g_b_out,
            g_first_gain,
            g_first_shift,
            table_local,
        ),
        "dp",
    )
    return (
        output,
        grad_tokens,
        g_table,
        g_first_gain,
        g_first_shift,
        g_w_query,
        g_b_query,
        g_w_key,
        g_w_value,
        g_b_value,
        g_w_out,
        g_b_out,
        g_second_gain,
        g_second_shift,
        g_w_in,
        g_b_in,
        g_w_down,
        g_b_down,
    )


def solution(mesh):
    in_specs = (
        P("dp", None, None),
        P("dp"),
        P("dp", None),
        P(),
        P(),
        P(),
        P(None, "tensor"),
        P("tensor"),
        P(None, "tensor"),
        P(None, "tensor"),
        P("tensor"),
        P("tensor", None),
        P(),
        P(),
        P(),
        P(None, "tensor"),
        P("tensor"),
        P("tensor", None),
        P(),
        P("dp", None, None),
    )
    out_specs = (
        P("dp", None, None),
        P("dp", None, None),
        P(),
        P(),
        P(),
        P(None, "tensor"),
        P("tensor"),
        P(None, "tensor"),
        P(None, "tensor"),
        P("tensor"),
        P("tensor", None),
        P(),
        P(),
        P(),
        P(None, "tensor"),
        P("tensor"),
        P("tensor", None),
        P(),
    )
    return jax.shard_map(
        per_device, mesh=mesh, in_specs=in_specs, out_specs=out_specs, check_vma=False
    )
```

profile of v0, /device:TPU:0, one launch (start us, length us, event | category | flops | bytes accessed | tf_op | source)
XLA Modules:
  0.0 734.9 jit_solution(14062246603834037431)
XLA Ops:
  9.7 2.2 fusion.55
  17.3 2.6 convolution_convert_fusion.5
  20.0 2.6 fusion.85
  22.6 25.1 %while.28 = (s32[]{:T(128)}, bf16[3,512,3,64]{1,3,2,0:T(8,128)(2,1)S(1)}, f32[3,3,512]{2,1,0:T(4,128)S(1)}, s32[3,512]{1,0:T(4,128)S(1)}, s32[3,512]{1,0:T(4,128...) while((s32[]{:T(128)}, ...), condition=%wide.region_6.7_spmd.clone, body=%wide.region_3.6_spmd.clone.sunk | while | flops 628456448 | bytes 33111156 | solution.py:114
  23.8 1.7 select_reduce_fusion.3
  25.6 2.6 fusion.171
  28.2 2.8 fusion.172
  32.2 1.7 select_reduce_fusion.3
  33.9 2.6 fusion.171
  36.6 2.8 fusion.172
  40.6 1.7 select_reduce_fusion.3
  42.3 2.6 fusion.171
  44.9 2.8 fusion.172
  48.5 3.4 convolution_convert_fusion.3
  52.8 57.6 %all-reduce.8.cloned.1.call-done = bf16[1536,768]{1,0:T(8,128)(2,1)} async-done(((bf16[1536,768]{1,0:T(8,128)(2,1)}), bf16[1536,768]{1,0:T(8,128)(2,1)}) %all-reduce.8.cloned.1.call-update) | async-done | bytes 2359312 | tf_op jit(solution)/shard_map/psum | solution.py:117
  110.4 3.5 fusion.99
  113.9 3.0 multiply_reduce_fusion.1
  117.0 1.8 add_convert_fusion.2
  120.2 2.1 fusion.103
  122.4 5.3 convert_reduce_fusion.3
  129.1 3.5 convolution_convert_fusion.1
  132.9 3.6 fusion.88
  136.5 7.2 convolution_convert_fusion.2
  143.7 44.8 %all-reduce.10.cloned.1.call-done = bf16[1536,768]{1,0:T(8,128)(2,1)} async-done(((bf16[1536,768]{1,0:T(8,128)(2,1)}), bf16[1536,768]{1,0:T(8,128)(2,1)}) %all-reduce.10.cloned.1.call-update) | async-done | bytes 2359312 | tf_op jit(solution)/shard_map/psum | solution.py:135
  188.5 6.4 fusion.82
  194.9 5.2 fusion.100
  200.2 2.2 copy-done.9
  202.4 1.8 convolution_convert_fusion.4
  207.4 72.0 %while.29 = (s32[]{:T(128)}, f32[1536,3,64]{0,2,1:T(8,128)}, f32[1536,3,64]{0,2,1:T(8,128)S(1)}, bf16[3,512,3,64]{1,3,2,0:T(8,128)(2,1)}, bf16[3,512,3,64]{1,3,2...) while((s32[]{:T(128)}, f32[1536,3,64]{0,2,1:T(8,128)}, ...), condition=%wide.region_16.17_spmd.clone, body=%wide.region_14.16_spmd.clone.sunk | while | flops 1542683648 | bytes 159318784 | solution.py:173
  208.9 1.4 fusion.182
  210.4 4.2 multiply_reduce_fusion.3
  214.6 4.0 multiply_convert_fusion.5
  218.6 4.4 fusion.184
  223.1 4.6 fusion.186
  227.7 3.7 fusion.185
  232.6 1.4 fusion.182
  234.1 4.2 multiply_reduce_fusion.3
  238.3 4.0 multiply_convert_fusion.5
  242.3 4.8 fusion.184
  247.1 4.6 fusion.186
  251.7 3.7 fusion.185
  256.6 1.4 fusion.182
  258.0 4.2 multiply_reduce_fusion.3
  262.3 4.0 multiply_convert_fusion.5
  266.3 4.8 fusion.184
  271.1 4.6 fusion.186
  275.7 3.7 fusion.185
  281.2 2.0 fusion.104
  284.3 2.3 add_convert_fusion
  286.9 6.1 fusion.106
  292.9 6.7 fusion.89
  299.6 1.4 fusion.107
  301.1 1.4 fusion.109
  302.5 1.4 fusion.108
  304.0 1.5 fusion.95
  305.5 75.6 %all-reduce.14.cloned.1.call-done = (bf16[1536,768]{1,0:T(8,128)(2,1)}, bf16[1536,768]{1,0:T(8,128)(2,1)}) async-done(((bf16[1536,768]{1,0:T(8,128)(2,1)}, bf16[1536,768]{1,0:T(8,128)(2,1)}), (bf16[1536,768]{1,0:T(8,128)(2,1)}, bf16[1536,768]{1,0:T(8,128)(2,1)})) %all-reduce.14.cloned.1.call-update) | async-done | bytes 4718608 | tf_op jit(solution)/shard_map/psum | solution.py:124
  381.1 4.6 fusion.83
  385.8 6.9 fusion.101
  392.7 1.9 broadcast_multiply_fusion
  396.0 39.6 %all-reduce = (f32[768]{0:T(1024)}, f32[768]{0:T(1024)}, f32[192]{0:T(256)}, f32[192]{0:T(256)}, f32[768]{0:T(1024)}, /*index=5*/f32[768]{0:T(1024)}, f32[768]{0:T(1024)}, f32[768]{0:T(1024)}, f32[768]{0:T(1024)}) all-reduce(f32[768]{0:T(1024)S(1)} %get-tuple-element.271, ...), channel_id=1, replica_groups=mesh['dp'=8,'tensor'=4] {'dp'}, use_global_device_ids=true, to_apply=%region_23.24 | all-reduce | flops 5760 | bytes 46080 | tf_op jit(solution)/shard_map/psum | solution.py:209
  435.6 282.6 %all-reduce.12.cloned.1.call-done = (f32[1000,768]{1,0:T(8,128)}, f32[768,192]{0,1:T(8,128)}, f32[768,192]{0,1:T(8,128)}, f32[768,192]{0,1:T(8,128)}, f32[192,76...) async-done(((f32[1000,768]{1,0:T(8,128)}, f32[768,192]{0,1:T(8,128)}, f32[768,192]{0,1:T(8,128)}, f32[768,192]{0,1:T(8,128)}, f32[192,768]{1,0:T(8,128)}, ...) | async-done | bytes 10149904 | tf_op jit(solution)/shard_map/psum | solution.py:209
  718.2 3.9 copy.89
  725.3 1.4 copy.94
  726.7 1.4 copy.95
  (219 shorter events, 29.7 us)
Async XLA Ops:
  7.2 2.1 copy-start
  7.2 5.7 copy-start.44
  7.2 5.7 copy-start.52
  7.2 103.2 %all-reduce.8.cloned.1.call-start = ((), (), s32[]{:S(2)}) async-start(), calls=%async_computation | async-start | bytes 4718592 | tf_op jit(solution)/shard_map/psum | solution.py:117
  7.3 4.6 copy-start.4
  9.6 6.1 copy-start.36
  9.7 6.0 copy-start.61
  11.9 120.9 %copy-start.34 = (f32[1536]{0:T(1024)}, f32[1536]{0:T(1024)S(1)}, u32[]{:S(2)}) copy-start(f32[1536]{0:T(1024)S(1)} %broadcast_multiply_fusion.7) | copy-start | bytes 18436
  12.9 119.9 %copy-start.41 = (f32[1536]{0:T(1024)}, f32[1536]{0:T(1024)S(1)}, u32[]{:S(2)}) copy-start(f32[1536]{0:T(1024)S(1)} %add_rsqrt_fusion.1) | copy-start | bytes 18436
  15.7 1.5 copy-start.37
  16.6 3.2 copy-start.56
  16.6 3.3 copy-start.39
  16.7 3.3 copy-start.62
  47.8 4.4 copy-start.11
  47.8 62.6 %copy-start.43 = (f32[768]{0:T(1024)S(1)}, f32[768]{0:T(1024)}, u32[]{:S(2)}) copy-start(f32[768]{0:T(1024)} %param.36) | copy-start | bytes 9220
  48.5 3.7 copy-start.16
  51.9 136.6 %all-reduce.10.cloned.1.call-start = ((), (), s32[]{:S(2)}) async-start(), calls=%async_computation.1 | async-start | bytes 4718592 | tf_op jit(solution)/shard_map/psum | solution.py:135
  52.8 64.2 %copy-start.46 = (f32[768]{0:T(1024)S(1)}, f32[768]{0:T(1024)}, u32[]{:S(2)}) copy-start(f32[768]{0:T(1024)} %param.37) | copy-start | bytes 9220
  52.8 64.2 %copy-start.53 = (f32[768]{0:T(1024)S(1)}, f32[768]{0:T(1024)}, u32[]{:S(2)}) copy-start(f32[768]{0:T(1024)} %param.38) | copy-start | bytes 9220
  110.4 3.5 copy-start.7
  110.4 6.6 copy-start.5
  117.0 3.3 copy-start.57
  120.2 2.1 copy-start.22
  120.2 2.1 copy-start.58
  120.2 2.1 copy-start.60
  122.4 5.3 copy-start.63
  132.6 248.5 %all-reduce.14.cloned.1.call-start = ((), (), s32[]{:S(2)}) async-start(), calls=%async_computation.3 | async-start | bytes 9437184 | tf_op jit(solution)/shard_map/psum | solution.py:124
  132.9 3.6 copy-start.59
  188.5 6.4 copy-start.6
  188.5 6.4 copy-start.8
  188.5 6.4 copy-start.15
  194.9 7.5 %copy-start.29 = (bf16[192,768]{1,0:T(8,128)(2,1)S(1)}, bf16[192,768]{1,0:T(8,128)(2,1)}, u32[]{:S(2)}) copy-start(bf16[192,768]{1,0:T(8,128)(2,1)} %param.35) | copy-start | bytes 884740
  200.2 2.2 copy-start.9
  210.4 4.3 copy-start.2
  218.6 9.1 %copy-start.3 = (f32[3,512,1536]{2,1,0:T(8,128)S(1)}, f32[3,512,1536]{2,1,0:T(8,128)}, u32[]{:S(2)}) copy-start(f32[3,512,1536]{2,1,0:T(8,128)} %copy-done.2) | copy-start | bytes 28311556 | tf_op jit(solution)/shard_map/while
  232.6 1.5 copy-start.12
  234.0 4.3 copy-start.2
  242.3 9.4 %copy-start.3 = (f32[3,512,1536]{2,1,0:T(8,128)S(1)}, f32[3,512,1536]{2,1,0:T(8,128)}, u32[]{:S(2)}) copy-start(f32[3,512,1536]{2,1,0:T(8,128)} %copy-done.2) | copy-start | bytes 28311556 | tf_op jit(solution)/shard_map/while
  258.0 4.3 copy-start.2
  266.3 9.4 %copy-start.3 = (f32[3,512,1536]{2,1,0:T(8,128)S(1)}, f32[3,512,1536]{2,1,0:T(8,128)}, u32[]{:S(2)}) copy-start(f32[3,512,1536]{2,1,0:T(8,128)} %copy-done.2) | copy-start | bytes 28311556 | tf_op jit(solution)/shard_map/while
  281.2 2.1 copy-start.19
  281.2 2.1 copy-start.10
  281.2 2.1 copy-start.38
  286.6 431.5 %all-reduce.12.cloned.1.call-start = ((), (), s32[]{:S(2)}) async-start(), calls=%async_computation.2 | async-start | bytes 20299776 | tf_op jit(solution)/shard_map/psum | solution.py:209
  286.8 6.1 copy-start.23
  292.9 6.7 copy-start.20
  292.9 6.7 copy-start.27
  299.6 4.3 slice-start
  301.1 2.9 slice-start.1
  301.1 2.9 copy-start.17
  302.5 78.6 %copy-start.35 = (f32[1536]{0:T(1024)S(1)}, f32[1536]{0:T(1024)}, u32[]{:S(2)}) copy-start(f32[1536]{0:T(1024)} %copy-done.34) | copy-start | bytes 18436
  302.5 78.6 %copy-start.42 = (f32[1536]{0:T(1024)S(1)}, f32[1536]{0:T(1024)}, u32[]{:S(2)}) copy-start(f32[1536]{0:T(1024)} %copy-done.41) | copy-start | bytes 18436
  302.5 78.6 %copy-start.45 = (f32[768]{0:T(1024)S(1)}, f32[768]{0:T(1024)}, u32[]{:S(2)}) copy-start(f32[768]{0:T(1024)} %param.28) | copy-start | bytes 9220
  304.0 81.8 %copy-start.54 = (f32[768]{0:T(1024)S(1)}, f32[768]{0:T(1024)}, u32[]{:S(2)}) copy-start(f32[768]{0:T(1024)} %param.42) | copy-start | bytes 9220
  381.1 4.7 copy-start.13
  381.1 4.7 copy-start.21
  385.8 6.9 copy-start.51
  718.2 3.9 copy-start.33
  718.2 4.7 copy-start.32
  718.2 5.5 copy-start.31
  718.2 6.3 copy-start.30
  718.2 7.1 copy-start.26
  722.0 4.7 copy-start.25
  724.5 3.6 copy-start.1
  (12 other events, 16.0 us)
Sparse Core Ops, SparseCore 0:
  52.0 58.3 all-reduce.7
  132.7 55.7 all-reduce.9
  286.7 94.2 all-reduce.13
  394.8 323.3 all-reduce.11
where the time goes:
time: 743 us; the launch traced here: 735 us
  waiting for transfers between devices  461 us (62%)
  matrix products  123 us (17%)
  other arithmetic  70.5 us (9%)
  blocking collectives  39.6 us (5%)
  local copies, waits for them, and re-layouts  24.2 us (3%)
  between operations  15.5 us (2%)
    psum x1, waiting for transfers between devices, per_device(): lax.psum((g_w_query, g_b_query, g_w_key, g_w_value, g_b_value, g_w_out, g...  283 us
    psum x1, waiting for transfers between devices, per_device(): lax.psum(mlp_part.astype(jnp.bfloat16), 'tensor').astype(jnp.float32)  75.6 us
    psum x1, waiting for transfers between devices, per_device(): lax.psum(attn_part.astype(jnp.bfloat16), 'tensor').astype(jnp.float32)  57.6 us
    psum x1, waiting for transfers between devices, per_device(): lax.psum(times_trans(grad_pre, w_in).astype(jnp.bfloat16), 'tensor')  44.8 us
    psum x1, blocking collectives, per_device(): lax.psum((g_w_query, g_b_query, g_w_key, g_w_value, g_b_value, g_w_out, g...  39.6 us
    unnamed x137, local copies, waits for them, and re-layouts  20.1 us
    dot_general x6, matrix products, inner_rows(): lax.dot_general(left, right, (((0,), (0,)), ((), ())), preferred_element_...  18.6 us
    dot_general x6, matrix products, times_trans(): lax.dot_general(left, right, (((1,), (1,)), ((), ())), preferred_element_...  15.7 us
  transfers between devices with their start and end apart: 4, of which 4 were waited for; matrix products, arithmetic and copies ran while one was open for 4% of the time, Pallas kernels for 0%

commit v1 on v0

--- a/solution.py
+++ b/solution.py
@@ -132,9 +132,9 @@
     grad_pre = gelu_pull(grad_active)[0].astype(jnp.bfloat16)
     g_b_in = jnp.sum(grad_pre.astype(jnp.float32), axis=0)
     g_w_in = inner_rows(normed_two, grad_pre)
-    grad_two = lax.psum(times_trans(grad_pre, w_in).astype(jnp.bfloat16), "tensor").astype(
-        jnp.float32
-    )
+    grad_two = jnp.sum(
+        lax.all_gather(times_trans(grad_pre, w_in).astype(jnp.bfloat16), "tensor"), axis=0
+    ).astype(jnp.float32)
     g_second_gain = jnp.sum(grad_two * hat_two, axis=0)
     g_second_shift = jnp.sum(grad_two, axis=0)
     g_w_in, g_b_in, g_w_down, g_b_down, g_second_gain, g_second_shift = lax.psum(

time: 743 us -> 761 us (1.024)
  other arithmetic: 70.5 us -> 79 us
  waiting for transfers between devices: 461 us -> 469 us
    all_gather x0 -> x1, waiting for transfers between devices: none -> 52.9 us  [per_device(): lax.all_gather(times_trans(grad_pre, w_in).astype(jnp.bfloat16), 'tensor')]
    psum x1 -> x0, waiting for transfers between devices: 44.8 us -> none  [per_device(): lax.psum(times_trans(grad_pre, w_in).astype(jnp.bfloat16), 'tensor')]
    unnamed x137 -> x135, local copies, waits for them, and re-layouts: 20.1 us -> 20.1 us
where the time goes in v1:
time: 761 us; the launch traced here: 752 us
  waiting for transfers between devices  469 us (62%)
  matrix products  123 us (16%)
  other arithmetic  79 us (10%)
  blocking collectives  39.6 us (5%)
  local copies, waits for them, and re-layouts  24.2 us (3%)
  between operations  15.5 us (2%)
    psum x1, waiting for transfers between devices, per_device(): lax.psum((g_w_query, g_b_query, g_w_key, g_w_value, g_b_value, g_w_out, g...  283 us
    psum x1, waiting for transfers between devices, per_device(): lax.psum(mlp_part.astype(jnp.bfloat16), 'tensor').astype(jnp.float32)  75.6 us
    psum x1, waiting for transfers between devices, per_device(): lax.psum(attn_part.astype(jnp.bfloat16), 'tensor').astype(jnp.float32)  58.2 us
    all_gather x1, waiting for transfers between devices, per_device(): lax.all_gather(times_trans(grad_pre, w_in).astype(jnp.bfloat16), 'tensor')  52.9 us
    psum x1, blocking collectives, per_device(): lax.psum((g_w_query, g_b_query, g_w_key, g_w_value, g_b_value, g_w_out, g...  39.6 us
    unnamed x135, local copies, waits for them, and re-layouts  20.1 us
    dot_general x6, matrix products, inner_rows(): lax.dot_general(left, right, (((0,), (0,)), ((), ())), preferred_element_...  18.5 us
    dot_general x6, matrix products, times_trans(): lax.dot_general(left, right, (((1,), (1,)), ((), ())), preferred_element_...  15.6 us
  transfers between devices with their start and end apart: 4, of which 4 were waited for; matrix products, arithmetic and copies ran while one was open for 4% of the time, Pallas kernels for 0%

profile of v1, /device:TPU:0, one launch (start us, length us, event | category | flops | bytes accessed | tf_op | source)
XLA Modules:
  0.0 751.9 jit_solution(17602325179279647837)
XLA Ops:
  9.7 2.2 fusion.55
  17.3 2.6 convolution_convert_fusion.5
  20.0 2.6 fusion.85
  22.6 25.1 %while.28 = (s32[]{:T(128)}, bf16[3,512,3,64]{1,3,2,0:T(8,128)(2,1)S(1)}, f32[3,3,512]{2,1,0:T(4,128)S(1)}, s32[3,512]{1,0:T(4,128)S(1)}, s32[3,512]{1,0:T(4,128...) while((s32[]{:T(128)}, ...), condition=%wide.region_6.7_spmd.clone, body=%wide.region_3.6_spmd.clone.sunk | while | flops 628456448 | bytes 33111156 | solution.py:114
  23.8 1.7 select_reduce_fusion.3
  25.6 2.6 fusion.171
  28.2 2.8 fusion.172
  32.2 1.7 select_reduce_fusion.3
  33.9 2.6 fusion.171
  36.6 2.8 fusion.172
  40.6 1.7 select_reduce_fusion.3
  42.3 2.6 fusion.171
  44.9 2.8 fusion.172
  48.5 3.4 convolution_convert_fusion.3
  52.2 58.2 %all-reduce.7.cloned.1.call-done = bf16[1536,768]{1,0:T(8,128)(2,1)} async-done(((bf16[1536,768]{1,0:T(8,128)(2,1)}), bf16[1536,768]{1,0:T(8,128)(2,1)}) %all-reduce.7.cloned.1.call-update) | async-done | bytes 2359312 | tf_op jit(solution)/shard_map/psum | solution.py:117
  110.4 3.5 fusion.99
  114.0 3.0 multiply_reduce_fusion.1
  117.0 3.1 add_convert_fusion.2
  121.6 2.1 fusion.103
  123.7 5.3 convert_reduce_fusion.3
  130.4 3.5 convolution_convert_fusion.1
  134.8 3.5 fusion.88
  138.3 7.2 convolution_convert_fusion.2
  145.5 52.9 %all-gather.3.cloned.1.call-done = bf16[6144,768]{1,0:T(8,128)(2,1)} async-done(((bf16[1536,768]{1,0:T(8,128)(2,1)}), bf16[6144,768]{1,0:T(8,128)(2,1)}) %all-gather.3.cloned.1.call-update) | async-done | bytes 9437200 | tf_op jit(solution)/shard_map/all_gather | solution.py:136
  198.4 7.1 reduce_sum.210
  205.5 6.4 fusion.82
  211.9 5.2 fusion.100
  217.2 2.2 copy-done.8
  219.4 1.7 convolution_convert_fusion.4
  224.3 72.2 %while.29 = (s32[]{:T(128)}, f32[1536,3,64]{0,2,1:T(8,128)}, f32[1536,3,64]{0,2,1:T(8,128)S(1)}, bf16[3,512,3,64]{1,3,2,0:T(8,128)(2,1)}, bf16[3,512,3,64]{1,3,2...) while((s32[]{:T(128)}, f32[1536,3,64]{0,2,1:T(8,128)}, ...), condition=%wide.region_16.17_spmd.clone, body=%wide.region_14.16_spmd.clone.sunk | while | flops 1542683648 | bytes 159318784 | solution.py:173
  225.9 1.4 fusion.182
  227.4 4.2 multiply_reduce_fusion.3
  231.6 4.1 multiply_convert_fusion.5
  235.7 4.4 fusion.184
  240.1 4.6 fusion.186
  244.8 3.7 fusion.185
  249.6 1.4 fusion.182
  251.1 4.2 multiply_reduce_fusion.3
  255.3 4.1 multiply_convert_fusion.5
  259.4 4.8 fusion.184
  264.2 4.6 fusion.186
  268.8 3.7 fusion.185
  273.7 1.4 fusion.182
  275.1 4.2 multiply_reduce_fusion.3
  279.4 4.1 multiply_convert_fusion.5
  283.4 4.8 fusion.184
  288.2 4.6 fusion.186
  292.8 3.7 fusion.185
  298.3 2.0 fusion.104
  301.5 2.3 add_convert_fusion
  304.0 6.0 fusion.106
  310.0 6.7 fusion.89
  316.7 1.4 fusion.107
  318.1 1.4 fusion.109
  319.6 1.4 fusion.108
  321.1 1.5 fusion.95
  322.6 75.6 %all-reduce.11.cloned.1.call-done = (bf16[1536,768]{1,0:T(8,128)(2,1)}, bf16[1536,768]{1,0:T(8,128)(2,1)}) async-done(((bf16[1536,768]{1,0:T(8,128)(2,1)}, bf16[1536,768]{1,0:T(8,128)(2,1)}), (bf16[1536,768]{1,0:T(8,128)(2,1)}, bf16[1536,768]{1,0:T(8,128)(2,1)})) %all-reduce.11.cloned.1.call-update) | async-done | bytes 4718608 | tf_op jit(solution)/shard_map/psum | solution.py:124
  398.2 4.6 fusion.83
  402.9 6.9 fusion.101
  409.8 1.9 broadcast_multiply_fusion
  413.1 39.6 %all-reduce = (f32[768]{0:T(1024)}, f32[768]{0:T(1024)}, f32[192]{0:T(256)}, f32[192]{0:T(256)}, f32[768]{0:T(1024)}, /*index=5*/f32[768]{0:T(1024)}, f32[768]{0:T(1024)}, f32[768]{0:T(1024)}, f32[768]{0:T(1024)}) all-reduce(f32[768]{0:T(1024)S(1)} %get-tuple-element.271, ...), channel_id=1, replica_groups=mesh['dp'=8,'tensor'=4] {'dp'}, use_global_device_ids=true, to_apply=%region_23.24 | all-reduce | flops 5760 | bytes 46080 | tf_op jit(solution)/shard_map/psum | solution.py:209
  452.6 282.6 %all-reduce.9.cloned.1.call-done = (f32[1000,768]{1,0:T(8,128)}, f32[768,192]{0,1:T(8,128)}, f32[768,192]{0,1:T(8,128)}, f32[768,192]{0,1:T(8,128)}, f32[192,768...) async-done(((f32[1000,768]{1,0:T(8,128)}, f32[768,192]{0,1:T(8,128)}, f32[768,192]{0,1:T(8,128)}, f32[768,192]{0,1:T(8,128)}, f32[192,768]{1,0:T(8,128)}, ...) | async-done | bytes 10149904 | tf_op jit(solution)/shard_map/psum | solution.py:209
  735.3 3.9 copy.89
  742.4 1.4 copy.94
  (218 shorter events, 31.1 us)
Async XLA Ops:
  7.2 2.1 copy-start
  7.2 5.7 copy-start.43
  7.2 5.7 copy-start.51
  7.2 103.2 %all-reduce.7.cloned.1.call-start = ((), (), s32[]{:S(2)}) async-start(), calls=%async_computation | async-start | bytes 4718592 | tf_op jit(solution)/shard_map/psum | solution.py:117
  7.3 4.6 copy-start.4
  9.6 6.1 copy-start.35
  9.7 6.0 copy-start.60
  11.9 122.9 %copy-start.33 = (f32[1536]{0:T(1024)}, f32[1536]{0:T(1024)S(1)}, u32[]{:S(2)}) copy-start(f32[1536]{0:T(1024)S(1)} %broadcast_multiply_fusion.7) | copy-start | bytes 18436
  12.9 121.9 %copy-start.40 = (f32[1536]{0:T(1024)}, f32[1536]{0:T(1024)S(1)}, u32[]{:S(2)}) copy-start(f32[1536]{0:T(1024)S(1)} %add_rsqrt_fusion.1) | copy-start | bytes 18436
  15.7 1.5 copy-start.36
  16.6 3.2 copy-start.55
  16.6 3.3 copy-start.38
  16.7 3.3 copy-start.61
  47.8 66.2 %copy-start.11 = (bf16[1536,3,64]{0,2,1:T(8,128)(2,1)}, bf16[1536,3,64]{0,2,1:T(8,128)(2,1)S(1)}, u32[]{:S(2)}) copy-start(bf16[1536,3,64]{0,2,1:T(8,128)(2,1)S(1)} %get-tuple-element.617) | copy-start | bytes 1769476
  47.8 62.6 %copy-start.42 = (f32[768]{0:T(1024)S(1)}, f32[768]{0:T(1024)}, u32[]{:S(2)}) copy-start(f32[768]{0:T(1024)} %param.36) | copy-start | bytes 9220
  48.5 65.5 %copy-start.15 = (bf16[24,8,3,512]{3,1,2,0:T(8,128)(2,1)}, bf16[24,8,3,512]{3,1,2,0:T(8,128)(2,1)S(1)}, u32[]{:S(2)}) copy-start(bf16[24,8,3,512]{3,1,2,0:T(8,128)(2,1)S(1)} %copy.51) | copy-start | bytes 1769476
  51.9 65.1 %copy-start.45 = (f32[768]{0:T(1024)S(1)}, f32[768]{0:T(1024)}, u32[]{:S(2)}) copy-start(f32[768]{0:T(1024)} %param.37) | copy-start | bytes 9220
  51.9 65.1 %copy-start.52 = (f32[768]{0:T(1024)S(1)}, f32[768]{0:T(1024)}, u32[]{:S(2)}) copy-start(f32[768]{0:T(1024)} %param.38) | copy-start | bytes 9220
  51.9 146.5 %all-gather.3.cloned.1.call-start = ((), (), s32[]{:S(2)}) async-start(), calls=%async_computation.1 | async-start | bytes 11796480 | tf_op jit(solution)/shard_map/all_gather | solution.py:136
  110.4 3.5 copy-start.6
  117.0 4.6 copy-start.56
  121.6 2.1 copy-start.21
  121.6 2.1 copy-start.57
  121.6 2.1 copy-start.59
  123.7 5.3 copy-start.62
  133.9 264.2 %all-reduce.11.cloned.1.call-start = ((), (), s32[]{:S(2)}) async-start(), calls=%async_computation.3 | async-start | bytes 9437184 | tf_op jit(solution)/shard_map/psum | solution.py:124
  134.2 4.1 copy-start.58
  205.5 6.4 copy-start.5
  205.5 6.4 copy-start.7
  205.5 6.4 copy-start.10
  211.9 7.5 copy-start.28
  217.2 2.2 copy-start.8
  227.4 4.3 copy-start.2
  235.7 9.1 %copy-start.3 = (f32[3,512,1536]{2,1,0:T(8,128)S(1)}, f32[3,512,1536]{2,1,0:T(8,128)}, u32[]{:S(2)}) copy-start(f32[3,512,1536]{2,1,0:T(8,128)} %copy-done.2) | copy-start | bytes 28311556 | tf_op jit(solution)/shard_map/while
  249.6 1.5 copy-start.12
  251.1 4.3 copy-start.2
  259.4 9.4 %copy-start.3 = (f32[3,512,1536]{2,1,0:T(8,128)S(1)}, f32[3,512,1536]{2,1,0:T(8,128)}, u32[]{:S(2)}) copy-start(f32[3,512,1536]{2,1,0:T(8,128)} %copy-done.2) | copy-start | bytes 28311556 | tf_op jit(solution)/shard_map/while
  273.6 1.5 copy-start.12
  275.1 4.3 copy-start.2
  283.4 9.4 %copy-start.3 = (f32[3,512,1536]{2,1,0:T(8,128)S(1)}, f32[3,512,1536]{2,1,0:T(8,128)}, u32[]{:S(2)}) copy-start(f32[3,512,1536]{2,1,0:T(8,128)} %copy-done.2) | copy-start | bytes 28311556 | tf_op jit(solution)/shard_map/while
  298.3 2.1 copy-start.18
  298.3 2.1 copy-start.9
  298.3 2.1 copy-start.37
  303.8 431.5 %all-reduce.9.cloned.1.call-start = ((), (), s32[]{:S(2)}) async-start(), calls=%async_computation.2 | async-start | bytes 20299776 | tf_op jit(solution)/shard_map/psum | solution.py:209
  304.0 6.0 copy-start.22
  310.0 6.7 copy-start.19
  310.0 6.7 copy-start.26
  316.7 4.4 slice-start
  318.1 2.9 slice-start.1
  318.1 2.9 copy-start.16
  319.6 78.6 %copy-start.34 = (f32[1536]{0:T(1024)S(1)}, f32[1536]{0:T(1024)}, u32[]{:S(2)}) copy-start(f32[1536]{0:T(1024)} %copy-done.33) | copy-start | bytes 18436
  319.6 78.6 %copy-start.41 = (f32[1536]{0:T(1024)S(1)}, f32[1536]{0:T(1024)}, u32[]{:S(2)}) copy-start(f32[1536]{0:T(1024)} %copy-done.40) | copy-start | bytes 18436
  319.6 78.6 %copy-start.44 = (f32[768]{0:T(1024)S(1)}, f32[768]{0:T(1024)}, u32[]{:S(2)}) copy-start(f32[768]{0:T(1024)} %param.28) | copy-start | bytes 9220
  321.1 81.8 %copy-start.53 = (f32[768]{0:T(1024)S(1)}, f32[768]{0:T(1024)}, u32[]{:S(2)}) copy-start(f32[768]{0:T(1024)} %param.42) | copy-start | bytes 9220
  398.2 4.7 copy-start.13
  398.2 4.7 copy-start.20
  402.8 6.9 copy-start.50
  735.2 3.9 copy-start.32
  735.3 4.7 copy-start.31
  735.3 5.5 copy-start.30
  735.3 6.3 copy-start.29
  735.3 7.1 copy-start.25
  739.1 4.7 copy-start.24
  741.6 3.6 copy-start.1
  (11 other events, 14.5 us)
Sparse Core Ops, SparseCore 0:
  52.0 58.3 all-reduce.6
  134.0 64.3 all-gather.2
  303.9 94.2 all-reduce.10
  411.9 323.3 all-reduce.8
